TPU v7x, 32 devices: a whole 2x2x4 slice. The times are simulated.
32 devices in a mesh: tile: 8 (over z, y), chan: 4 (over x, core).
Axes of the slice: x: 2, y: 2, z: 4, core: 2. Of those that a mesh axis runs over, the one named last changes fastest.
Arguments:
- feat: bfloat16 [128, 64, 256], P('tile', 'chan'), may hold values from -6 to 6
- lift: float32 [64], replicated, may hold values from -3 to 3
- dilation4_weight: bfloat16 [3, 3, 64, 64], replicated, may hold values from -0.25 to 0.25
- dilation8_weight: bfloat16 [3, 3, 64, 64], replicated, may hold values from -0.25 to 0.25
- entry_fraction: bfloat16 [2048, 128], P('tile'), may hold values from 0.019897461 to 0.19921875
- entry_target_tile: int32 [2048, 1], P('tile'), may hold values from 0 to 7; in each aligned block of 256 rows (0 to 255, 256 to 511, ...) at most 64 rows name the same one
- entry_owner_tile: int32 [2048], P('tile'), may hold values from 0 to 31
- entry_local_net: int32 [2048], P('tile'), may hold values from 0 to 63
- pin_demand_weight: float32 [2048], P('tile'), may hold values from 0.2 to 2
- pin_local_net: int32 [2048], P('tile'), may hold values from 0 to 63
- pin_global_cell: int32 [2048], P('tile'), may hold values from 0 to 511
Outputs:
- cell_grad: float32 [512], P('tile')
Inputs may be any that keep to these rules, and one draw needn't show every extreme that they name: `entry_target_tile`: among the entries of one tile index, at most 64 name the same destination, and in some tile index exactly 64 do.
All inputs are finite; a program needn't handle non-finite values.
Results may differ from a plain program's by a relative error of at most 0.0003.
Values may be sent and summed in bfloat16 or wider, within the bound.
A program may use at most 64 MiB of HBM per device.

v0:
```python
import jax
import jax.numpy as jnp
from jax import lax
from jax.sharding import PartitionSpec as P

NET_DEV = 64
CELL_DEV = 64
TILE_DEV = 32


def extended(array, sides, width):
    for axis, dim in sides:
        peers, length = (lax.axis_size(axis), array.shape[dim])
        up = [(i, (i + 1) % peers) for i in range(peers - 1)]
        down = [(j, i) for i, j in up]
        last = lax.slice_in_dim(array, length - width, length, axis=dim)
        leading = lax.slice_in_dim(array, 0, width, axis=dim)
        before = lax.ppermute(last, axis, up)
        after = lax.ppermute(leading, axis, down)
        array = jnp.concatenate([before, array, after], axis=dim)
    return array


def flipped_kernel(kernel):
    return jnp.transpose(kernel[::-1, ::-1], (0, 1, 3, 2))


def dilated_convolution(own_part, weights, channel_start, dilation):
    row_count, chan_own, col_count = own_part.shape
    rimmed = extended(own_part, (("tile", 0),), dilation)
    own_weights = lax.dynamic_slice_in_dim(weights, channel_start, chan_own, 3)
    start_sum = jnp.zeros((row_count, chan_own, col_count), jnp.float32)
    running = start_sum
    widened = jnp.pad(
        lax.all_gather(rimmed, "chan", axis=1, tiled=True), ((0, 0), (0, 0), (dilation, dilation))
    )
    for row_tap in range(3):
        for col_tap in range(3):
            part_in = widened[
                row_tap * dilation : row_tap * dilation + row_count,
                :,
                col_tap * dilation : col_tap * dilation + col_count,
            ]
            running = running + jnp.einsum(
                "rcw,co->row",
                part_in,
                own_weights[row_tap, col_tap],
                preferred_element_type=jnp.float32,
            )
    return running


def local(
    feat,
    lift,
    dilation4_weight,
    dilation8_weight,
    entry_fraction,
    entry_target_tile,
    entry_owner_tile,
    entry_local_net,
    pin_demand_weight,
    pin_local_net,
    pin_global_cell,
):
    highest = lax.Precision.HIGHEST
    tile_count = lax.axis_size("tile")
    chan_count = lax.axis_size("chan")
    row_count, chan_own, col_count = feat.shape
    channel_start = lax.axis_index("chan") * chan_own
    lift_own = lax.dynamic_slice_in_dim(lift, channel_start, chan_own, 0)
    entry_count = entry_target_tile.shape[0]
    capacity = chan_count * max(1, 2 * entry_count // (chan_count * tile_count))
    part_total = 1
    part_id = 0
    slot_count = capacity // part_total
    destination = entry_target_tile[:, 0]
    dest_hot = (destination[:, None] == jnp.arange(tile_count, dtype=jnp.int32)[None, :]).astype(
        jnp.int32
    )
    rank = jnp.sum(jnp.cumsum(dest_hot, axis=0) * dest_hot, axis=1) - 1
    placed = rank % part_total == part_id
    slot_row = jnp.where(
        placed, destination * slot_count + rank // part_total, tile_count * slot_count
    )
    pin_hot = (pin_local_net[None, :] == jnp.arange(NET_DEV, dtype=jnp.int32)[:, None]).astype(
        jnp.float32
    )
    strength = jnp.dot(pin_hot, pin_demand_weight, precision=highest)
    entry_hot = (entry_local_net[:, None] == jnp.arange(NET_DEV, dtype=jnp.int32)[None, :]).astype(
        jnp.float32
    )
    entry_strength = jnp.dot(entry_hot, strength, precision=highest)
    frac = entry_fraction.astype(jnp.float32)
    payload = entry_strength[:, None] * frac
    send_rows = (
        jnp.zeros((tile_count * slot_count, 128), jnp.float32)
        .at[slot_row]
        .set(payload, mode="drop")
    )
    send_ids = (
        jnp.zeros((tile_count * slot_count,), jnp.int32)
        .at[slot_row]
        .set(entry_owner_tile, mode="drop")
    )
    arrived, arrived_ids = (
        lax.all_to_all(
            send_rows.reshape(tile_count, slot_count, 128).astype(jnp.bfloat16),
            "tile",
            split_axis=0,
            concat_axis=0,
            tiled=True,
        ).astype(jnp.float32),
        lax.all_to_all(
            send_ids.reshape(tile_count, slot_count),
            "tile",
            split_axis=0,
            concat_axis=0,
            tiled=True,
        ),
    )
    tile_hot = (
        arrived_ids.reshape(-1)[:, None] == jnp.arange(TILE_DEV, dtype=jnp.int32)[None, :]
    ).astype(jnp.float32)
    tiles = jnp.dot(tile_hot.T, arrived.reshape(-1, 128), precision=highest)
    demand = (
        tiles.reshape(row_count // 8, col_count // 16, 8, 16)
        .transpose(0, 2, 1, 3)
        .reshape(row_count, col_count)
    )
    input_features = (
        feat.astype(jnp.float32) + demand[:, None, :] * lift_own[None, :, None]
    ).astype(jnp.bfloat16)
    first_preactivation = dilated_convolution(input_features, dilation4_weight, channel_start, 4)
    hidden_features = jax.nn.silu(first_preactivation).astype(jnp.bfloat16)
    second_output = dilated_convolution(hidden_features, dilation8_weight, channel_start, 8)
    second_gradient = jax.nn.sigmoid(second_output).astype(jnp.bfloat16)
    hidden_gradient = dilated_convolution(
        second_gradient, flipped_kernel(dilation8_weight), channel_start, 8
    )
    sigmoid_pre = jax.nn.sigmoid(first_preactivation)
    preactivation_gradient = (
        hidden_gradient * sigmoid_pre * (1.0 + first_preactivation * (1.0 - sigmoid_pre))
    ).astype(jnp.bfloat16)
    inputs_gradient = dilated_convolution(
        preactivation_gradient, flipped_kernel(dilation4_weight), channel_start, 4
    )
    partial_grad = jnp.sum(inputs_gradient * lift_own[None, :, None], axis=1)
    grad_demand = lax.psum(partial_grad, "chan")
    grad_tiles = (
        grad_demand.reshape(row_count // 8, 8, col_count // 16, 16)
        .transpose(0, 2, 1, 3)
        .reshape(TILE_DEV, 128)
    )
    slot_grads = jnp.dot(tile_hot, grad_tiles, precision=highest).reshape(
        tile_count, slot_count, 128
    )
    returned = lax.all_to_all(
        slot_grads.astype(jnp.bfloat16), "tile", split_axis=0, concat_axis=0, tiled=True
    ).astype(slot_grads.dtype)
    entry_rows = jnp.take(returned.reshape(-1, 128), slot_row, axis=0, mode="fill", fill_value=0.0)
    entry_grad = jnp.sum(entry_rows * frac, axis=1)
    grad_net = jnp.dot(entry_grad, entry_hot, precision=highest)
    pin_grad = jnp.dot(grad_net, pin_hot, precision=highest)
    cell_term = jax.ops.segment_sum(pin_grad, pin_global_cell, num_segments=CELL_DEV * tile_count)
    return lax.psum_scatter(cell_term, "tile", scatter_dimension=0, tiled=True)


def solution(mesh):
    in_specs = (
        P("tile", "chan", None),
        P(),
        P(),
        P(),
        P("tile", None),
        P("tile", None),
        P("tile"),
        P("tile"),
        P("tile"),
        P("tile"),
        P("tile"),
    )
    out_specs = P("tile")
    return jax.shard_map(local, mesh=mesh, in_specs=in_specs, out_specs=out_specs, check_vma=False)
```

profile of v0, /device:TPU:0, one launch (start us, length us, event | category | flops | bytes accessed | tf_op | source)
XLA Modules:
  0.0 194.8 jit_solution(14243430125302070767)
XLA Ops:
  9.6 1.6 scatter_custom_fusion
  11.8 7.3 %all-to-all-start = ((s32[8,1,64]{2,1,0:T(1,128)}), s32[8,1,64]{2,1,0:T(1,128)S(1)}, u32[]{:S(2)}, u32[]{:S(2)}) async-start(s32[8,1,64]{2,1,0:T(1,128)} %all_to_all.12), calls=%async_computation | async-start | bytes 8192 | tf_op jit(solution)/shard_map/all_to_all | solution.py:114
  19.9 0.9 fusion.42
  20.8 1.7 scatter_custom_fusion.1
  23.2 2.4 %all-to-all-done = s32[8,1,64]{2,1,0:T(1,128)S(1)} async-done(((s32[8,1,64]{2,1,0:T(1,128)}), s32[8,1,64]{2,1,0:T(1,128)S(1)}, u32[]{:S(2)}, u32[]{:S(2)}) %all-to-all-start) | async-done | bytes 2080 | tf_op jit(solution)/shard_map/all_to_all | solution.py:114
  25.6 3.6 %all-to-all-start.1 = ((bf16[8,64,128]{2,1,0:T(8,128)(2,1)}), bf16[8,64,128]{2,1,0:T(8,128)(2,1)S(1)}, u32[]{:S(2)}, u32[]{:S(2)}) async-start(bf16[8,64,128]{2,1,0:T(8,128)(2,1)} %bitcast.24), calls=%async_computation.1 | async-start | bytes 262144 | tf_op jit(solution)/shard_map/all_to_all | solution.py:107
  30.5 5.9 %all-to-all-done.1 = bf16[8,64,128]{2,1,0:T(8,128)(2,1)S(1)} async-done(((bf16[8,64,128]{2,1,0:T(8,128)(2,1)}), bf16[8,64,128]{2,1,0:T(8,128)(2,1)S(1)}, u32[]{:S(2)}, u32[]{:S(2)}) %all-to-all-start.1) | async-done | bytes 131104 | tf_op jit(solution)/shard_map/all_to_all | solution.py:107
  37.2 1.3 collective-permute-start.1
  38.5 4.5 %collective-permute-start = (bf16[4,16,256]{2,1,0:T(8,128)(2,1)S(1)}, bf16[4,16,256]{2,1,0:T(8,128)(2,1)S(1)}, u32[]{:S(2)}, u32[]{:S(2)}) collective-permute-start(bf16[4,16,256]{2,1,0:T(8,128)(2,1)S(1)} %get-tuple-element.13), channel_id=1, source_target_pairs={{0,4},{4,8},{8,12},{12,16},{16,20},{20,24},{24,28},{1,5},{5,9},{9,... | collective-permute-start | bytes 98312 | tf_op jit(solution)/shard_map/ppermute | solution.py:18
  43.1 1.6 collective-permute-done
  44.7 8.6 %all_gather.12 = bf16[24,64,256]{2,1,0:T(8,128)(2,1)S(1)} all-gather(bf16[24,16,256]{2,1,0:T(8,128)(2,1)S(1)} %pad_maximum_fusion.2), channel_id=1, replica_groups=mesh['tile'=8,'chan'=4] {'chan'}, dimensions={1}, use_global_device_ids=true | all-gather | bytes 983040 | tf_op jit(solution)/shard_map/all_gather | solution.py:35
  56.4 1.3 collective-permute-start.3
  57.7 4.9 %collective-permute-start.2 = (bf16[8,16,256]{2,1,0:T(8,128)(2,1)S(1)}, bf16[8,16,256]{2,1,0:T(8,128)(2,1)S(1)}, u32[]{:S(2)}, u32[]{:S(2)}) collective-permute-start(bf16[8,16,256]{2,1,0:T(8,128)(2,1)S(1)} %get-tuple-element.11), channel_id=1, source_target_pairs={{0,4},{4,8},{8,12},{12,16},{16,20},{20,24},{24,28},{1,5},{5,9},{9,... | collective-permute-start | bytes 196616 | tf_op jit(solution)/shard_map/ppermute | solution.py:18
  63.2 1.6 collective-permute-done.2
  65.6 17.1 %all-gather.3.cloned.1.call-done = bf16[32,64,256]{2,1,0:T(8,128)(2,1)} async-done(((bf16[32,16,256]{2,1,0:T(8,128)(2,1)}), bf16[32,64,256]{2,1,0:T(8,128)(2,1)}) %all-gather.3.cloned.1.call-update) | async-done | bytes 1048592 | tf_op jit(solution)/shard_map/all_gather | solution.py:35
  82.7 1.5 fusion.33
  86.9 1.6 fusion.46
  88.6 1.3 collective-permute-start.5
  89.9 4.7 %collective-permute-start.4 = (bf16[8,16,256]{2,0,1:T(8,128)(2,1)S(1)}, bf16[8,16,256]{2,0,1:T(8,128)(2,1)S(1)}, u32[]{:S(2)}, u32[]{:S(2)}) collective-permute-start(bf16[8,16,256]{2,0,1:T(8,128)(2,1)S(1)} %get-tuple-element.9), channel_id=1, source_target_pairs={{0,4},{4,8},{8,12},{12,16},{16,20},{20,24},{24,28},{1,5},{5,9},{9,... | collective-permute-start | bytes 196616 | tf_op jit(solution)/shard_map/ppermute | solution.py:18
  94.7 1.6 collective-permute-done.4
  97.2 18.6 %all-gather.5.cloned.1.call-done = bf16[32,64,256]{2,0,1:T(8,128)(2,1)} async-done(((bf16[32,16,256]{2,0,1:T(8,128)(2,1)}), bf16[32,64,256]{2,0,1:T(8,128)(2,1)}) %all-gather.5.cloned.1.call-update) | async-done | bytes 1048592 | tf_op jit(solution)/shard_map/all_gather | solution.py:35
  115.7 1.8 copy.66
  120.1 1.3 collective-permute-start.7
  121.4 4.5 %collective-permute-start.6 = (bf16[4,16,256]{2,1,0:T(8,128)(2,1)S(1)}, bf16[4,16,256]{2,1,0:T(8,128)(2,1)S(1)}, u32[]{:S(2)}, u32[]{:S(2)}) collective-permute-start(bf16[4,16,256]{2,1,0:T(8,128)(2,1)S(1)} %get-tuple-element.7), channel_id=1, source_target_pairs={{0,4},{4,8},{8,12},{12,16},{16,20},{20,24},{24,28},{1,5},{5,9},{9,... | collective-permute-start | bytes 98312 | tf_op jit(solution)/shard_map/ppermute | solution.py:18
  126.0 1.5 collective-permute-done.6
  127.6 7.5 %all_gather.15 = bf16[24,64,256]{2,1,0:T(8,128)(2,1)S(1)} all-gather(bf16[24,16,256]{2,1,0:T(8,128)(2,1)S(1)} %pad_maximum_fusion.3), channel_id=1, replica_groups=mesh['tile'=8,'chan'=4] {'chan'}, dimensions={1}, use_global_device_ids=true | all-gather | bytes 983040 | tf_op jit(solution)/shard_map/all_gather | solution.py:35
  137.8 11.7 %psum.7 = f32[32,128]{1,0:T(8,128)S(1)} all-reduce(f32[32,128]{1,0:T(8,128)S(1)} %reshape.105), channel_id=1, replica_groups=mesh['tile'=8,'chan'=4] {'chan'}, use_global_device_ids=true, to_apply=%region_6.7 | all-reduce | flops 4096 | bytes 32768 | tf_op jit(solution)/shard_map/psum | solution.py:149
  149.6 1.0 convolution_convert_fusion
  150.6 7.4 %all-to-all-start.2 = ((bf16[8,64,128]{2,1,0:T(8,128)(2,1)}), bf16[8,64,128]{2,1,0:T(8,128)(2,1)S(1)}, u32[]{:S(2)}, u32[]{:S(2)}) async-start(bf16[8,64,128]{2,1,0:T(8,128)(2,1)} %convolution_convert_fusion), calls=%async_computation.2 | async-start | bytes 262144 | tf_op jit(solution)/shard_map/all_to_all | solution.py:158
  159.3 6.1 %all-to-all-done.2 = bf16[8,64,128]{2,1,0:T(8,128)(2,1)S(1)} async-done(((bf16[8,64,128]{2,1,0:T(8,128)(2,1)}), bf16[8,64,128]{2,1,0:T(8,128)(2,1)S(1)}, u32[]{:S(2)}, u32[]{:S(2)}) %all-to-all-start.2) | async-done | bytes 131104 | tf_op jit(solution)/shard_map/all_to_all | solution.py:158
  166.7 2.5 %scatter_custom_fusion.2 = f32[512]{0:T(512)S(1)} fusion(s32[256]{0:T(256)} %param.21, f32[256]{0:T(256)S(1)} %bitcast.284, f32[]{:T(128)} %constant.62.clone.1), kind=kCustom, calls=%fused_computation.201 | custom fusion | flops 256 | bytes 2560 | tf_op jit(solution)/shard_map/scatter-add | solution.py:165
  169.2 18.2 %all-reduce.4 = f32[512]{0:T(512)S(1)} all-reduce(f32[512]{0:T(512)S(1)} %scatter_custom_fusion.2), channel_id=2, replica_groups=mesh['tile'=8,'chan'=4] {'tile'}, use_global_device_ids=true, to_apply=%region_9.10.clone | all-reduce | flops 512 | bytes 4096
  (106 shorter events, 23.3 us)
Async XLA Ops:
  6.5 12.6 %copy-start = (f32[256]{0:T(256)S(1)}, f32[256]{0:T(256)}, u32[]{:S(2)}) copy-start(f32[256]{0:T(256)} %param.19) | copy-start | bytes 3076
  6.5 22.7 %copy-start.8 = (f32[64]{0:T(128)S(1)}, f32[64]{0:T(128)}, u32[]{:S(2)}) copy-start(f32[64]{0:T(128)} %param.12) | copy-start | bytes 772
  6.5 30.5 %copy-start.5 = (bf16[16,16,256]{2,1,0:T(8,128)(2,1)S(1)}, bf16[16,16,256]{2,1,0:T(8,128)(2,1)}, u32[]{:S(2)}) copy-start(bf16[16,16,256]{2,1,0:T(8,128)(2,1)} %param.11) | copy-start | bytes 393220
  11.8 13.8 %all-to-all-start = ((s32[8,1,64]{2,1,0:T(1,128)}), s32[8,1,64]{2,1,0:T(1,128)S(1)}, u32[]{:S(2)}, u32[]{:S(2)}) async-start(s32[8,1,64]{2,1,0:T(1,128)} %all_to_all.12), calls=%async_computation | async-start | bytes 8192 | tf_op jit(solution)/shard_map/all_to_all | solution.py:114
  25.6 10.9 %all-to-all-start.1 = ((bf16[8,64,128]{2,1,0:T(8,128)(2,1)}), bf16[8,64,128]{2,1,0:T(8,128)(2,1)S(1)}, u32[]{:S(2)}, u32[]{:S(2)}) async-start(bf16[8,64,128]{2,1,0:T(8,128)(2,1)} %bitcast.24), calls=%async_computation.1 | async-start | bytes 262144 | tf_op jit(solution)/shard_map/all_to_all | solution.py:107
  29.2 53.6 %all-gather.3.cloned.1.call-start = ((), (), s32[]{:S(2)}) async-start(), calls=%async_computation.3 | async-start | bytes 1310720 | tf_op jit(solution)/shard_map/all_gather | solution.py:35
  36.6 16.7 %copy-start.3 = (bf16[3,3,64,64]{3,2,1,0:T(8,128)(2,1)S(1)}, bf16[3,3,64,64]{3,2,1,0:T(8,128)(2,1)}, u32[]{:S(2)}) copy-start(bf16[3,3,64,64]{3,2,1,0:T(8,128)(2,1)} %param.13) | copy-start | bytes 221188
  37.2 5.9 %collective-permute-start.1 = (bf16[4,16,256]{2,1,0:T(8,128)(2,1)S(1)}, bf16[4,16,256]{2,1,0:T(8,128)(2,1)S(1)}, u32[]{:S(2)}, u32[]{:S(2)}) collective-permute-start(bf16[4,16,256]{2,1,0:T(8,128)(2,1)S(1)} %get-tuple-element.14), channel_id=1, source_target_pairs={{4,0},{8,4},{12,8},{16,12},{20,16},{24,20},{28,24},{5,1},{9,5},{13... | collective-permute-start | bytes 98312 | tf_op jit(solution)/shard_map/ppermute | solution.py:19
  38.5 6.1 %collective-permute-start = (bf16[4,16,256]{2,1,0:T(8,128)(2,1)S(1)}, bf16[4,16,256]{2,1,0:T(8,128)(2,1)S(1)}, u32[]{:S(2)}, u32[]{:S(2)}) collective-permute-start(bf16[4,16,256]{2,1,0:T(8,128)(2,1)S(1)} %get-tuple-element.13), channel_id=1, source_target_pairs={{0,4},{4,8},{8,12},{12,16},{16,20},{20,24},{24,28},{1,5},{5,9},{9,... | collective-permute-start | bytes 98312 | tf_op jit(solution)/shard_map/ppermute | solution.py:18
  56.0 26.7 %copy-start.2 = (bf16[3,3,64,64]{3,2,1,0:T(8,128)(2,1)S(1)}, bf16[3,3,64,64]{3,2,1,0:T(8,128)(2,1)}, u32[]{:S(2)}) copy-start(bf16[3,3,64,64]{3,2,1,0:T(8,128)(2,1)} %param.14) | copy-start | bytes 221188
  56.4 6.8 %collective-permute-start.3 = (bf16[8,16,256]{2,1,0:T(8,128)(2,1)S(1)}, bf16[8,16,256]{2,1,0:T(8,128)(2,1)S(1)}, u32[]{:S(2)}, u32[]{:S(2)}) collective-permute-start(bf16[8,16,256]{2,1,0:T(8,128)(2,1)S(1)} %get-tuple-element.12), channel_id=1, source_target_pairs={{4,0},{8,4},{12,8},{16,12},{20,16},{24,20},{28,24},{5,1},{9,5},{13... | collective-permute-start | bytes 196616 | tf_op jit(solution)/shard_map/ppermute | solution.py:19
  57.7 7.1 %collective-permute-start.2 = (bf16[8,16,256]{2,1,0:T(8,128)(2,1)S(1)}, bf16[8,16,256]{2,1,0:T(8,128)(2,1)S(1)}, u32[]{:S(2)}, u32[]{:S(2)}) collective-permute-start(bf16[8,16,256]{2,1,0:T(8,128)(2,1)S(1)} %get-tuple-element.11), channel_id=1, source_target_pairs={{0,4},{4,8},{8,12},{12,16},{16,20},{20,24},{24,28},{1,5},{5,9},{9,... | collective-permute-start | bytes 196616 | tf_op jit(solution)/shard_map/ppermute | solution.py:18
  65.6 50.2 %all-gather.5.cloned.1.call-start = ((), (), s32[]{:S(2)}) async-start(), calls=%async_computation.4 | async-start | bytes 1310720 | tf_op jit(solution)/shard_map/all_gather | solution.py:35
  82.7 1.5 copy-start.1
  88.6 6.2 %collective-permute-start.5 = (bf16[8,16,256]{2,0,1:T(8,128)(2,1)S(1)}, bf16[8,16,256]{2,0,1:T(8,128)(2,1)S(1)}, u32[]{:S(2)}, u32[]{:S(2)}) collective-permute-start(bf16[8,16,256]{2,0,1:T(8,128)(2,1)S(1)} %get-tuple-element.10), channel_id=1, source_target_pairs={{4,0},{8,4},{12,8},{16,12},{20,16},{24,20},{28,24},{5,1},{9,5},{13... | collective-permute-start | bytes 196616 | tf_op jit(solution)/shard_map/ppermute | solution.py:19
  89.9 6.4 %collective-permute-start.4 = (bf16[8,16,256]{2,0,1:T(8,128)(2,1)S(1)}, bf16[8,16,256]{2,0,1:T(8,128)(2,1)S(1)}, u32[]{:S(2)}, u32[]{:S(2)}) collective-permute-start(bf16[8,16,256]{2,0,1:T(8,128)(2,1)S(1)} %get-tuple-element.9), channel_id=1, source_target_pairs={{0,4},{4,8},{8,12},{12,16},{16,20},{20,24},{24,28},{1,5},{5,9},{9,... | collective-permute-start | bytes 196616 | tf_op jit(solution)/shard_map/ppermute | solution.py:18
  120.1 5.9 %collective-permute-start.7 = (bf16[4,16,256]{2,1,0:T(8,128)(2,1)S(1)}, bf16[4,16,256]{2,1,0:T(8,128)(2,1)S(1)}, u32[]{:S(2)}, u32[]{:S(2)}) collective-permute-start(bf16[4,16,256]{2,1,0:T(8,128)(2,1)S(1)} %get-tuple-element.8), channel_id=1, source_target_pairs={{4,0},{8,4},{12,8},{16,12},{20,16},{24,20},{28,24},{5,1},{9,5},{13... | collective-permute-start | bytes 98312 | tf_op jit(solution)/shard_map/ppermute | solution.py:19
  121.4 6.1 %collective-permute-start.6 = (bf16[4,16,256]{2,1,0:T(8,128)(2,1)S(1)}, bf16[4,16,256]{2,1,0:T(8,128)(2,1)S(1)}, u32[]{:S(2)}, u32[]{:S(2)}) collective-permute-start(bf16[4,16,256]{2,1,0:T(8,128)(2,1)S(1)} %get-tuple-element.7), channel_id=1, source_target_pairs={{0,4},{4,8},{8,12},{12,16},{16,20},{20,24},{24,28},{1,5},{5,9},{9,... | collective-permute-start | bytes 98312 | tf_op jit(solution)/shard_map/ppermute | solution.py:18
  137.2 20.8 %copy-start.9 = (u32[32]{0:T(128)S(1)}, u32[32]{0:T(128)}, u32[]{:S(2)}) copy-start(u32[32]{0:T(128)} %constant.82) | copy-start | bytes 388
  137.8 28.3 %copy-start.4 = (bf16[256,128]{1,0:T(8,128)(2,1)S(1)}, bf16[256,128]{1,0:T(8,128)(2,1)}, u32[]{:S(2)}) copy-start(bf16[256,128]{1,0:T(8,128)(2,1)} %param.15) | copy-start | bytes 196612
  150.6 15.7 %copy-start.6 = (s32[256]{0:T(256)S(1)}, s32[256]{0:T(256)}, u32[]{:S(2)}) copy-start(s32[256]{0:T(256)} %param.18) | copy-start | bytes 3076
  150.6 15.9 %copy-start.7 = (s32[256]{0:T(256)S(1)}, s32[256]{0:T(256)}, u32[]{:S(2)}) copy-start(s32[256]{0:T(256)} %param.20) | copy-start | bytes 3076
  150.6 14.7 %all-to-all-start.2 = ((bf16[8,64,128]{2,1,0:T(8,128)(2,1)}), bf16[8,64,128]{2,1,0:T(8,128)(2,1)S(1)}, u32[]{:S(2)}, u32[]{:S(2)}) async-start(bf16[8,64,128]{2,1,0:T(8,128)(2,1)} %convolution_convert_fusion), calls=%async_computation.2 | async-start | bytes 262144 | tf_op jit(solution)/shard_map/all_to_all | solution.py:158
Sparse Core Ops, SparseCore 0:
  65.7 16.9 all-gather.2
  97.2 18.4 all-gather.4
where the time goes:
time: 196 us; the launch traced here: 195 us
  waiting for transfers between devices  57.2 us (29%)
  blocking collectives  46 us (23%)
  starting transfers between devices  42.2 us (22%)
  matrix products  15.8 us (8%)
  between operations  14.4 us (7%)
  other arithmetic  11.8 us (6%)
  local copies, waits for them, and re-layouts  7.41 us (4%)
    all_gather x2, waiting for transfers between devices, dilated_convolution(): lax.all_gather(rimmed, 'chan', axis=1, tiled=True)  35.7 us
    ppermute x4, starting transfers between devices, extended(): before = lax.ppermute(last, axis, up)  18.7 us
    unnamed x1, blocking collectives  18.2 us
    all_gather x2, blocking collectives, dilated_convolution(): lax.all_gather(rimmed, 'chan', axis=1, tiled=True)  16.1 us
    dot_general x36, matrix products, dilated_convolution(): jnp.einsum('rcw,co->row', part_in, own_weights[row_tap, col_tap], preferr...  12.4 us
    psum x1, blocking collectives, local(): grad_demand = lax.psum(partial_grad, 'chan')  11.7 us
    all_to_all x1, starting transfers between devices, local(): lax.all_to_all(slot_grads.astype(jnp.bfloat16), 'tile', split_axis=0, con...  7.38 us
    all_to_all x1, starting transfers between devices, local(): lax.all_to_all(send_ids.reshape(tile_count, slot_count), 'tile', split_ax...  7.31 us
  transfers between devices with their start and end apart: 13, of which 11 were waited for; matrix products, arithmetic and copies ran while one was open for 3% of the time, Pallas kernels for 0%

commit v1 on v0

--- a/solution.py
+++ b/solution.py
@@ -146,7 +146,7 @@
         preactivation_gradient, flipped_kernel(dilation4_weight), channel_start, 4
     )
     partial_grad = jnp.sum(inputs_gradient * lift_own[None, :, None], axis=1)
-    grad_demand = lax.psum(partial_grad, "chan")
+    grad_demand = jnp.sum(lax.all_gather(partial_grad, "chan"), axis=0)
     grad_tiles = (
         grad_demand.reshape(row_count // 8, 8, col_count // 16, 16)
         .transpose(0, 2, 1, 3)

time: 196 us -> 190 us (0.969)
  blocking collectives: 46 us -> 39.8 us
    psum x1 -> x0, blocking collectives: 11.7 us -> none  [local(): grad_demand = lax.psum(partial_grad, 'chan')]
    all_gather x0 -> x1, blocking collectives: none -> 5.24 us  [local(): grad_demand = jnp.sum(lax.all_gather(partial_grad, 'chan'), axis=0)]
where the time goes in v1:
time: 190 us; the launch traced here: 189 us
  waiting for transfers between devices  57.4 us (30%)
  starting transfers between devices  42.4 us (22%)
  blocking collectives  39.8 us (21%)
  matrix products  15.8 us (8%)
  between operations  14.4 us (8%)
  other arithmetic  11.8 us (6%)
  local copies, waits for them, and re-layouts  7.41 us (4%)
    all_gather x2, waiting for transfers between devices, dilated_convolution(): lax.all_gather(rimmed, 'chan', axis=1, tiled=True)  35.7 us
    ppermute x4, starting transfers between devices, extended(): before = lax.ppermute(last, axis, up)  18.7 us
    unnamed x1, blocking collectives  18.6 us
    all_gather x2, blocking collectives, dilated_convolution(): lax.all_gather(rimmed, 'chan', axis=1, tiled=True)  16.1 us
    dot_general x36, matrix products, dilated_convolution(): jnp.einsum('rcw,co->row', part_in, own_weights[row_tap, col_tap], preferr...  12.4 us
    all_to_all x1, starting transfers between devices, local(): lax.all_to_all(slot_grads.astype(jnp.bfloat16), 'tile', split_axis=0, con...  7.59 us
    all_to_all x1, starting transfers between devices, local(): lax.all_to_all(send_ids.reshape(tile_count, slot_count), 'tile', split_ax...  7.31 us
    ppermute x4, waiting for transfers between devices, extended(): before = lax.ppermute(last, axis, up)  6.25 us
  transfers between devices with their start and end apart: 13, of which 11 were waited for; matrix products, arithmetic and copies ran while one was open for 3% of the time, Pallas kernels for 0%

profile of v1, /device:TPU:0, one launch (start us, length us, event | category | flops | bytes accessed | tf_op | source)
XLA Modules:
  0.0 189.0 jit_solution(1828485017414091264)
XLA Ops:
  9.6 1.6 scatter_custom_fusion
  11.8 7.3 %all-to-all-start = ((s32[8,1,64]{2,1,0:T(1,128)}), s32[8,1,64]{2,1,0:T(1,128)S(1)}, u32[]{:S(2)}, u32[]{:S(2)}) async-start(s32[8,1,64]{2,1,0:T(1,128)} %all_to_all.12), calls=%async_computation | async-start | bytes 8192 | tf_op jit(solution)/shard_map/all_to_all | solution.py:114
  19.9 0.9 fusion.42
  20.8 1.7 scatter_custom_fusion.1
  23.2 2.4 %all-to-all-done = s32[8,1,64]{2,1,0:T(1,128)S(1)} async-done(((s32[8,1,64]{2,1,0:T(1,128)}), s32[8,1,64]{2,1,0:T(1,128)S(1)}, u32[]{:S(2)}, u32[]{:S(2)}) %all-to-all-start) | async-done | bytes 2080 | tf_op jit(solution)/shard_map/all_to_all | solution.py:114
  25.6 3.6 %all-to-all-start.1 = ((bf16[8,64,128]{2,1,0:T(8,128)(2,1)}), bf16[8,64,128]{2,1,0:T(8,128)(2,1)S(1)}, u32[]{:S(2)}, u32[]{:S(2)}) async-start(bf16[8,64,128]{2,1,0:T(8,128)(2,1)} %bitcast.24), calls=%async_computation.1 | async-start | bytes 262144 | tf_op jit(solution)/shard_map/all_to_all | solution.py:107
  30.5 5.9 %all-to-all-done.1 = bf16[8,64,128]{2,1,0:T(8,128)(2,1)S(1)} async-done(((bf16[8,64,128]{2,1,0:T(8,128)(2,1)}), bf16[8,64,128]{2,1,0:T(8,128)(2,1)S(1)}, u32[]{:S(2)}, u32[]{:S(2)}) %all-to-all-start.1) | async-done | bytes 131104 | tf_op jit(solution)/shard_map/all_to_all | solution.py:107
  37.2 1.3 collective-permute-start.1
  38.5 4.5 %collective-permute-start = (bf16[4,16,256]{2,1,0:T(8,128)(2,1)S(1)}, bf16[4,16,256]{2,1,0:T(8,128)(2,1)S(1)}, u32[]{:S(2)}, u32[]{:S(2)}) collective-permute-start(bf16[4,16,256]{2,1,0:T(8,128)(2,1)S(1)} %get-tuple-element.13), channel_id=1, source_target_pairs={{0,4},{4,8},{8,12},{12,16},{16,20},{20,24},{24,28},{1,5},{5,9},{9,... | collective-permute-start | bytes 98312 | tf_op jit(solution)/shard_map/ppermute | solution.py:18
  43.1 1.6 collective-permute-done
  44.7 8.6 %all_gather.18 = bf16[24,64,256]{2,1,0:T(8,128)(2,1)S(1)} all-gather(bf16[24,16,256]{2,1,0:T(8,128)(2,1)S(1)} %pad_maximum_fusion.2), channel_id=1, replica_groups=mesh['tile'=8,'chan'=4] {'chan'}, dimensions={1}, use_global_device_ids=true | all-gather | bytes 983040 | tf_op jit(solution)/shard_map/all_gather | solution.py:35
  56.4 1.3 collective-permute-start.3
  57.7 4.9 %collective-permute-start.2 = (bf16[8,16,256]{2,1,0:T(8,128)(2,1)S(1)}, bf16[8,16,256]{2,1,0:T(8,128)(2,1)S(1)}, u32[]{:S(2)}, u32[]{:S(2)}) collective-permute-start(bf16[8,16,256]{2,1,0:T(8,128)(2,1)S(1)} %get-tuple-element.11), channel_id=1, source_target_pairs={{0,4},{4,8},{8,12},{12,16},{16,20},{20,24},{24,28},{1,5},{5,9},{9,... | collective-permute-start | bytes 196616 | tf_op jit(solution)/shard_map/ppermute | solution.py:18
  63.2 1.6 collective-permute-done.2
  65.6 17.1 %all-gather.4.cloned.1.call-done = bf16[32,64,256]{2,1,0:T(8,128)(2,1)} async-done(((bf16[32,16,256]{2,1,0:T(8,128)(2,1)}), bf16[32,64,256]{2,1,0:T(8,128)(2,1)}) %all-gather.4.cloned.1.call-update) | async-done | bytes 1048592 | tf_op jit(solution)/shard_map/all_gather | solution.py:35
  82.7 1.5 fusion.33
  86.9 1.6 fusion.46
  88.6 1.3 collective-permute-start.5
  89.9 4.7 %collective-permute-start.4 = (bf16[8,16,256]{2,0,1:T(8,128)(2,1)S(1)}, bf16[8,16,256]{2,0,1:T(8,128)(2,1)S(1)}, u32[]{:S(2)}, u32[]{:S(2)}) collective-permute-start(bf16[8,16,256]{2,0,1:T(8,128)(2,1)S(1)} %get-tuple-element.9), channel_id=1, source_target_pairs={{0,4},{4,8},{8,12},{12,16},{16,20},{20,24},{24,28},{1,5},{5,9},{9,... | collective-permute-start | bytes 196616 | tf_op jit(solution)/shard_map/ppermute | solution.py:18
  94.7 1.6 collective-permute-done.4
  97.2 18.6 %all-gather.6.cloned.1.call-done = bf16[32,64,256]{2,0,1:T(8,128)(2,1)} async-done(((bf16[32,16,256]{2,0,1:T(8,128)(2,1)}), bf16[32,64,256]{2,0,1:T(8,128)(2,1)}) %all-gather.6.cloned.1.call-update) | async-done | bytes 1048592 | tf_op jit(solution)/shard_map/all_gather | solution.py:35
  115.7 1.8 copy.104
  120.1 1.3 collective-permute-start.7
  121.4 4.5 %collective-permute-start.6 = (bf16[4,16,256]{2,1,0:T(8,128)(2,1)S(1)}, bf16[4,16,256]{2,1,0:T(8,128)(2,1)S(1)}, u32[]{:S(2)}, u32[]{:S(2)}) collective-permute-start(bf16[4,16,256]{2,1,0:T(8,128)(2,1)S(1)} %get-tuple-element.7), channel_id=1, source_target_pairs={{0,4},{4,8},{8,12},{12,16},{16,20},{20,24},{24,28},{1,5},{5,9},{9,... | collective-permute-start | bytes 98312 | tf_op jit(solution)/shard_map/ppermute | solution.py:18
  126.0 1.5 collective-permute-done.6
  127.6 7.5 %all_gather.21 = bf16[24,64,256]{2,1,0:T(8,128)(2,1)S(1)} all-gather(bf16[24,16,256]{2,1,0:T(8,128)(2,1)S(1)} %pad_maximum_fusion.3), channel_id=1, replica_groups=mesh['tile'=8,'chan'=4] {'chan'}, dimensions={1}, use_global_device_ids=true | all-gather | bytes 983040 | tf_op jit(solution)/shard_map/all_gather | solution.py:35
  137.6 5.2 %all-gather = f32[64,256]{1,0:T(8,128)S(1)} all-gather(f32[16,256]{1,0:T(8,128)S(1)} %fusion.6), channel_id=2, replica_groups=mesh['tile'=8,'chan'=4] {'chan'}, dimensions={0}, use_global_device_ids=true | all-gather | bytes 81920 | tf_op jit(solution)/shard_map/all_gather | solution.py:149
  143.1 1.0 convolution_convert_fusion
  144.1 7.6 %all-to-all-start.2 = ((bf16[8,64,128]{2,1,0:T(8,128)(2,1)}), bf16[8,64,128]{2,1,0:T(8,128)(2,1)S(1)}, u32[]{:S(2)}, u32[]{:S(2)}) async-start(bf16[8,64,128]{2,1,0:T(8,128)(2,1)} %convolution_convert_fusion), calls=%async_computation.2 | async-start | bytes 262144 | tf_op jit(solution)/shard_map/all_to_all | solution.py:158
  153.0 6.2 %all-to-all-done.2 = bf16[8,64,128]{2,1,0:T(8,128)(2,1)S(1)} async-done(((bf16[8,64,128]{2,1,0:T(8,128)(2,1)}), bf16[8,64,128]{2,1,0:T(8,128)(2,1)S(1)}, u32[]{:S(2)}, u32[]{:S(2)}) %all-to-all-start.2) | async-done | bytes 131104 | tf_op jit(solution)/shard_map/all_to_all | solution.py:158
  160.5 2.5 %scatter_custom_fusion.2 = f32[512]{0:T(512)S(1)} fusion(s32[256]{0:T(256)} %param.21, f32[256]{0:T(256)S(1)} %bitcast.284, f32[]{:T(128)} %constant.62.clone.1), kind=kCustom, calls=%fused_computation.200 | custom fusion | flops 256 | bytes 2560 | tf_op jit(solution)/shard_map/scatter-add | solution.py:165
  163.0 18.6 %all-reduce.4 = f32[512]{0:T(512)S(1)} all-reduce(f32[512]{0:T(512)S(1)} %scatter_custom_fusion.2), channel_id=3, replica_groups=mesh['tile'=8,'chan'=4] {'tile'}, use_global_device_ids=true, to_apply=%region_9.10.clone | all-reduce | flops 512 | bytes 4096
  (107 shorter events, 23.3 us)
Async XLA Ops:
  6.5 12.6 %copy-start = (f32[256]{0:T(256)S(1)}, f32[256]{0:T(256)}, u32[]{:S(2)}) copy-start(f32[256]{0:T(256)} %param.19) | copy-start | bytes 3076
  6.5 22.7 %copy-start.8 = (f32[64]{0:T(128)S(1)}, f32[64]{0:T(128)}, u32[]{:S(2)}) copy-start(f32[64]{0:T(128)} %param.12) | copy-start | bytes 772
  6.5 30.5 %copy-start.5 = (bf16[16,16,256]{2,1,0:T(8,128)(2,1)S(1)}, bf16[16,16,256]{2,1,0:T(8,128)(2,1)}, u32[]{:S(2)}) copy-start(bf16[16,16,256]{2,1,0:T(8,128)(2,1)} %param.11) | copy-start | bytes 393220
  11.8 13.8 %all-to-all-start = ((s32[8,1,64]{2,1,0:T(1,128)}), s32[8,1,64]{2,1,0:T(1,128)S(1)}, u32[]{:S(2)}, u32[]{:S(2)}) async-start(s32[8,1,64]{2,1,0:T(1,128)} %all_to_all.12), calls=%async_computation | async-start | bytes 8192 | tf_op jit(solution)/shard_map/all_to_all | solution.py:114
  25.6 10.9 %all-to-all-start.1 = ((bf16[8,64,128]{2,1,0:T(8,128)(2,1)}), bf16[8,64,128]{2,1,0:T(8,128)(2,1)S(1)}, u32[]{:S(2)}, u32[]{:S(2)}) async-start(bf16[8,64,128]{2,1,0:T(8,128)(2,1)} %bitcast.24), calls=%async_computation.1 | async-start | bytes 262144 | tf_op jit(solution)/shard_map/all_to_all | solution.py:107
  29.2 53.6 %all-gather.4.cloned.1.call-start = ((), (), s32[]{:S(2)}) async-start(), calls=%async_computation.3 | async-start | bytes 1310720 | tf_op jit(solution)/shard_map/all_gather | solution.py:35
  36.6 16.7 %copy-start.3 = (bf16[3,3,64,64]{3,2,1,0:T(8,128)(2,1)S(1)}, bf16[3,3,64,64]{3,2,1,0:T(8,128)(2,1)}, u32[]{:S(2)}) copy-start(bf16[3,3,64,64]{3,2,1,0:T(8,128)(2,1)} %param.13) | copy-start | bytes 221188
  37.2 5.9 %collective-permute-start.1 = (bf16[4,16,256]{2,1,0:T(8,128)(2,1)S(1)}, bf16[4,16,256]{2,1,0:T(8,128)(2,1)S(1)}, u32[]{:S(2)}, u32[]{:S(2)}) collective-permute-start(bf16[4,16,256]{2,1,0:T(8,128)(2,1)S(1)} %get-tuple-element.14), channel_id=1, source_target_pairs={{4,0},{8,4},{12,8},{16,12},{20,16},{24,20},{28,24},{5,1},{9,5},{13... | collective-permute-start | bytes 98312 | tf_op jit(solution)/shard_map/ppermute | solution.py:19
  38.5 6.1 %collective-permute-start = (bf16[4,16,256]{2,1,0:T(8,128)(2,1)S(1)}, bf16[4,16,256]{2,1,0:T(8,128)(2,1)S(1)}, u32[]{:S(2)}, u32[]{:S(2)}) collective-permute-start(bf16[4,16,256]{2,1,0:T(8,128)(2,1)S(1)} %get-tuple-element.13), channel_id=1, source_target_pairs={{0,4},{4,8},{8,12},{12,16},{16,20},{20,24},{24,28},{1,5},{5,9},{9,... | collective-permute-start | bytes 98312 | tf_op jit(solution)/shard_map/ppermute | solution.py:18
  56.0 26.7 %copy-start.2 = (bf16[3,3,64,64]{3,2,1,0:T(8,128)(2,1)S(1)}, bf16[3,3,64,64]{3,2,1,0:T(8,128)(2,1)}, u32[]{:S(2)}) copy-start(bf16[3,3,64,64]{3,2,1,0:T(8,128)(2,1)} %param.14) | copy-start | bytes 221188
  56.4 6.8 %collective-permute-start.3 = (bf16[8,16,256]{2,1,0:T(8,128)(2,1)S(1)}, bf16[8,16,256]{2,1,0:T(8,128)(2,1)S(1)}, u32[]{:S(2)}, u32[]{:S(2)}) collective-permute-start(bf16[8,16,256]{2,1,0:T(8,128)(2,1)S(1)} %get-tuple-element.12), channel_id=1, source_target_pairs={{4,0},{8,4},{12,8},{16,12},{20,16},{24,20},{28,24},{5,1},{9,5},{13... | collective-permute-start | bytes 196616 | tf_op jit(solution)/shard_map/ppermute | solution.py:19
  57.7 7.1 %collective-permute-start.2 = (bf16[8,16,256]{2,1,0:T(8,128)(2,1)S(1)}, bf16[8,16,256]{2,1,0:T(8,128)(2,1)S(1)}, u32[]{:S(2)}, u32[]{:S(2)}) collective-permute-start(bf16[8,16,256]{2,1,0:T(8,128)(2,1)S(1)} %get-tuple-element.11), channel_id=1, source_target_pairs={{0,4},{4,8},{8,12},{12,16},{16,20},{20,24},{24,28},{1,5},{5,9},{9,... | collective-permute-start | bytes 196616 | tf_op jit(solution)/shard_map/ppermute | solution.py:18
  65.6 50.2 %all-gather.6.cloned.1.call-start = ((), (), s32[]{:S(2)}) async-start(), calls=%async_computation.4 | async-start | bytes 1310720 | tf_op jit(solution)/shard_map/all_gather | solution.py:35
  82.7 1.5 copy-start.1
  88.6 6.2 %collective-permute-start.5 = (bf16[8,16,256]{2,0,1:T(8,128)(2,1)S(1)}, bf16[8,16,256]{2,0,1:T(8,128)(2,1)S(1)}, u32[]{:S(2)}, u32[]{:S(2)}) collective-permute-start(bf16[8,16,256]{2,0,1:T(8,128)(2,1)S(1)} %get-tuple-element.10), channel_id=1, source_target_pairs={{4,0},{8,4},{12,8},{16,12},{20,16},{24,20},{28,24},{5,1},{9,5},{13... | collective-permute-start | bytes 196616 | tf_op jit(solution)/shard_map/ppermute | solution.py:19
  89.9 6.4 %collective-permute-start.4 = (bf16[8,16,256]{2,0,1:T(8,128)(2,1)S(1)}, bf16[8,16,256]{2,0,1:T(8,128)(2,1)S(1)}, u32[]{:S(2)}, u32[]{:S(2)}) collective-permute-start(bf16[8,16,256]{2,0,1:T(8,128)(2,1)S(1)} %get-tuple-element.9), channel_id=1, source_target_pairs={{0,4},{4,8},{8,12},{12,16},{16,20},{20,24},{24,28},{1,5},{5,9},{9,... | collective-permute-start | bytes 196616 | tf_op jit(solution)/shard_map/ppermute | solution.py:18
  120.1 5.9 %collective-permute-start.7 = (bf16[4,16,256]{2,1,0:T(8,128)(2,1)S(1)}, bf16[4,16,256]{2,1,0:T(8,128)(2,1)S(1)}, u32[]{:S(2)}, u32[]{:S(2)}) collective-permute-start(bf16[4,16,256]{2,1,0:T(8,128)(2,1)S(1)} %get-tuple-element.8), channel_id=1, source_target_pairs={{4,0},{8,4},{12,8},{16,12},{20,16},{24,20},{28,24},{5,1},{9,5},{13... | collective-permute-start | bytes 98312 | tf_op jit(solution)/shard_map/ppermute | solution.py:19
  121.4 6.1 %collective-permute-start.6 = (bf16[4,16,256]{2,1,0:T(8,128)(2,1)S(1)}, bf16[4,16,256]{2,1,0:T(8,128)(2,1)S(1)}, u32[]{:S(2)}, u32[]{:S(2)}) collective-permute-start(bf16[4,16,256]{2,1,0:T(8,128)(2,1)S(1)} %get-tuple-element.7), channel_id=1, source_target_pairs={{0,4},{4,8},{8,12},{12,16},{16,20},{20,24},{24,28},{1,5},{5,9},{9,... | collective-permute-start | bytes 98312 | tf_op jit(solution)/shard_map/ppermute | solution.py:18
  137.2 14.5 %copy-start.9 = (u32[32]{0:T(128)S(1)}, u32[32]{0:T(128)}, u32[]{:S(2)}) copy-start(u32[32]{0:T(128)} %constant.82) | copy-start | bytes 388
  143.1 16.9 %copy-start.4 = (bf16[256,128]{1,0:T(8,128)(2,1)S(1)}, bf16[256,128]{1,0:T(8,128)(2,1)}, u32[]{:S(2)}) copy-start(bf16[256,128]{1,0:T(8,128)(2,1)} %param.15) | copy-start | bytes 196612
  144.1 16.0 %copy-start.6 = (s32[256]{0:T(256)S(1)}, s32[256]{0:T(256)}, u32[]{:S(2)}) copy-start(s32[256]{0:T(256)} %param.18) | copy-start | bytes 3076
  144.1 16.3 %copy-start.7 = (s32[256]{0:T(256)S(1)}, s32[256]{0:T(256)}, u32[]{:S(2)}) copy-start(s32[256]{0:T(256)} %param.20) | copy-start | bytes 3076
  144.1 15.1 %all-to-all-start.2 = ((bf16[8,64,128]{2,1,0:T(8,128)(2,1)}), bf16[8,64,128]{2,1,0:T(8,128)(2,1)S(1)}, u32[]{:S(2)}, u32[]{:S(2)}) async-start(bf16[8,64,128]{2,1,0:T(8,128)(2,1)} %convolution_convert_fusion), calls=%async_computation.2 | async-start | bytes 262144 | tf_op jit(solution)/shard_map/all_to_all | solution.py:158
Sparse Core Ops, SparseCore 0:
  65.7 16.9 all-gather.3
  97.2 18.4 all-gather.5
